TPU v7x, 256 devices: a whole 4x4x8 slice. The times are simulated.
256 devices in a mesh: strike: 64 (over y, z, core), dip: 4 (over x).
Axes of the slice: x: 4, y: 4, z: 8, core: 2. Of those that a mesh axis runs over, the one named last changes fastest.
Arguments:
- slip_rate: float32 [3, 4096, 1024], P(None, 'strike', 'dip'), may hold values from -6 to 6
- history: bfloat16 [4, 3, 2, 1024, 4096], P(None, None, None, ('strike', 'dip')), may hold values from -6 to 6
- lengths: int32 [1024, 4096], P(('strike', 'dip')), may hold values from 1 to 4, as said below
- prestress: float32 [2, 4096, 1024], P(None, 'strike', 'dip'), may hold values from -8 to 8
- normal_stress: float32 [4096, 1024], P('strike', 'dip'), may hold values from 8 to 16
- direct_effect: float32 [4096, 1024], P('strike', 'dip'), may hold values from 0.01 to 0.04
- state_log: float32 [4096, 1024], P('strike', 'dip'), may hold values from 1 to 5
Outputs:
- next_rates: float32 [3, 4096, 1024], P(None, 'strike', 'dip')
- next_state: float32 [4096, 1024], P('strike', 'dip')
Inputs may be any that keep to these rules, and one draw needn't show every extreme that they name: `lengths`: how many of the newest slip-rate spectra enter each wavenumber's stress transfer.
All inputs are finite; a program needn't handle non-finite values.
Results may differ from a plain program's by a relative error of at most 0.0003.
Values sent between devices are 32-bit elements; how exact they have to be, the bound alone decides.
No kernel may reach another device: no remote copies, remote signals or barrier semaphores. Data moves between devices by JAX's collectives and lax.ppermute only.
A program may use at most 128 MiB of HBM per device.

v0:
```python
import math
import jax
import jax.numpy as jnp
from jax import lax
from jax.sharding import PartitionSpec as P

HIST = 4
NEWTON = 2
time_step = 0.5
coupling = 0.5
decay_rate = 0.05
shear_speed = 0.6
opening_speed = 1.7
radiation = 0.5
healing = 1.0
slip_length = 2.0
highest = lax.Precision.HIGHEST


def area_sine(ratio):
    return jnp.log(ratio + jnp.sqrt(ratio * ratio + 1.0))


def wave_geometry(dip_modes, strike_modes, dip_cells, strike_cells):
    signed_dip = jnp.where(2 * dip_modes < dip_cells, dip_modes, dip_modes - dip_cells)
    signed_strike = jnp.where(
        2 * strike_modes < strike_cells, strike_modes, strike_modes - strike_cells
    )
    wave_dip = signed_dip.astype(jnp.float32) * (2.0 * math.pi / dip_cells)
    wave_strike = signed_strike.astype(jnp.float32) * (2.0 * math.pi / strike_cells)
    modulus = jnp.sqrt(wave_strike * wave_strike + wave_dip * wave_dip)
    anchor = (signed_dip == 0) & (signed_strike == 0)
    safe_modulus = jnp.where(anchor, 1.0, modulus)
    unit_strike = jnp.where(anchor, 1.0, wave_strike / safe_modulus)
    unit_dip = jnp.where(anchor, 0.0, wave_dip / safe_modulus)
    return (modulus, unit_strike, unit_dip)


def delay_mixing(geometry, delay):
    modulus, unit_strike, unit_dip = geometry
    phase_arg = modulus * (time_step * (delay + 1.0))
    envelope = -coupling * time_step * modulus * jnp.exp(-decay_rate * phase_arg)
    mode_two = envelope * jnp.cos(phase_arg)
    mode_three = envelope * jnp.cos(shear_speed * phase_arg)
    mode_one = envelope * jnp.cos(opening_speed * phase_arg)
    mix_along = unit_strike * unit_strike * mode_two + unit_dip * unit_dip * mode_three
    mix_cross = unit_strike * unit_dip * (mode_two - mode_three)
    mix_across = unit_dip * unit_dip * mode_two + unit_strike * unit_strike * mode_three
    return (mix_along, mix_cross, mix_across, mode_one)


def delay_term(spectrum, mixing, active):
    mix_along, mix_cross, mix_across, mode_one = mixing
    force_strike = (mix_along * spectrum[0] + mix_cross * spectrum[1]) * active
    force_dip = (mix_cross * spectrum[0] + mix_across * spectrum[1]) * active
    force_open = mode_one * spectrum[2] * active
    return jnp.stack([force_strike, force_dip, force_open])


def friction_step(force_field, prestress, normal_stress, direct_effect, state_log):
    load_strike = prestress[0] + force_field[0]
    load_dip = prestress[1] + force_field[1]
    traction = jnp.sqrt(load_strike * load_strike + load_dip * load_dip)
    strength = direct_effect * normal_stress
    factor = 2.0 * radiation * jnp.exp(-state_log)
    estimate = jnp.minimum(traction / strength, area_sine(traction / factor))
    for repeat in range(NEWTON):
        residual = traction - strength * estimate - factor * jnp.sinh(estimate)
        estimate = estimate + residual / (strength + factor * jnp.cosh(estimate))
    slip_speed = (traction - strength * estimate) / radiation
    unit_scale = slip_speed / jnp.maximum(traction, 1.0)
    new_rates = jnp.stack(
        [unit_scale * load_strike, unit_scale * load_dip, force_field[2] / radiation]
    )
    new_state = state_log + time_step * (healing * jnp.exp(-state_log) - slip_speed / slip_length)
    return (new_rates, new_state)


def phase_table(first_index, second_index, period):
    turn_count = first_index[:, None] * second_index[None, :] % period
    angle_table = turn_count.astype(jnp.float32) * (2.0 * math.pi / period)
    return (jnp.cos(angle_table), jnp.sin(angle_table))


def contract(pattern, first_operand, second_operand):
    return jnp.einsum(pattern, first_operand, second_operand, precision=highest)


def pair_section(part_real, part_imag, pattern, cos_table, sin_table, sign):
    out_real = contract(pattern, part_real, cos_table) - sign * contract(
        pattern, part_imag, sin_table
    )
    out_imag = contract(pattern, part_imag, cos_table) + sign * contract(
        pattern, part_real, sin_table
    )
    return (out_real, out_imag)


def twist_phase(part_real, part_imag, cos_table, sin_table, sign):
    out_real = cos_table * part_real - sign * sin_table * part_imag
    out_imag = cos_table * part_imag + sign * sin_table * part_real
    return (out_real, out_imag)


def shards(slip_rate, history, lengths, prestress, normal_stress, direct_effect, state_log):
    strike_count = lax.axis_size("strike")
    dip_count = lax.axis_size("dip")
    strike_index = lax.axis_index("strike")
    dip_index = lax.axis_index("dip")
    row_count = slip_rate.shape[1]
    dip_block = slip_rate.shape[2]
    mode_rows = history.shape[3]
    strike_cells = history.shape[4]
    dip_cells = dip_block * dip_count
    unit_modes = dip_count * mode_rows
    norm_dip = 1.0 / math.sqrt(dip_cells)
    norm_strike = 1.0 / math.sqrt(strike_cells)
    local_modes = jnp.arange(mode_rows, dtype=jnp.int32)
    dip_modes = (strike_index * dip_count + dip_index) * mode_rows + local_modes
    strike_modes = jnp.arange(strike_cells, dtype=jnp.int32)
    geometry = wave_geometry(dip_modes[:, None], strike_modes[None, :], dip_cells, strike_cells)
    coarse_all = jnp.arange(unit_modes, dtype=jnp.int32)
    coarse_own = dip_index * mode_rows + local_modes
    outer_index = jnp.arange(strike_count, dtype=jnp.int32)
    inner_index = jnp.arange(row_count, dtype=jnp.int32)
    cos_outer, sin_outer = phase_table(outer_index, outer_index, strike_count)
    cos_bend, sin_bend = phase_table(outer_index, inner_index, strike_cells)
    cos_bend = cos_bend * norm_strike
    sin_bend = sin_bend * norm_strike
    cos_inner, sin_inner = phase_table(inner_index, inner_index, row_count)

    def strike_forward(spectral):
        item_count = spectral.shape[0]
        grid_view = spectral.reshape(item_count, 2, mode_rows, strike_count, row_count)
        section_real, section_imag = pair_section(
            grid_view[:, 0], grid_view[:, 1], "ngpr,kp->ngkr", cos_outer, sin_outer, -1.0
        )
        bent_real, bent_imag = twist_phase(section_real, section_imag, cos_bend, sin_bend, -1.0)
        out_real, out_imag = pair_section(
            bent_real, bent_imag, "ngkr,rm->ngmk", cos_inner, sin_inner, -1.0
        )
        return jnp.stack([out_real, out_imag], axis=1).reshape(
            item_count, 2, mode_rows, strike_cells
        )

    def strike_inverse(spectral):
        grid_view = spectral.reshape(3, 2, mode_rows, row_count, strike_count)
        section_real, section_imag = pair_section(
            grid_view[:, 0], grid_view[:, 1], "ngmk,rm->ngrk", cos_inner, sin_inner, 1.0
        )
        bent_real, bent_imag = twist_phase(section_real, section_imag, cos_bend.T, sin_bend.T, 1.0)
        out_real, out_imag = pair_section(
            bent_real, bent_imag, "ngrk,kp->ngpr", cos_outer, sin_outer, 1.0
        )
        return jnp.stack([out_real, out_imag], axis=1).reshape(3, 2, mode_rows, strike_cells)

    def to_modes(space_field):
        gathered = lax.all_gather(space_field, "dip", axis=2, tiled=True)
        cos_first, sin_first = phase_table(coarse_all, coarse_own, unit_modes)
        cos_twist, sin_twist = phase_table(outer_index, coarse_own, dip_cells)
        grid_view = gathered.reshape(3, row_count, unit_modes, strike_count)
        first_real = contract("cxab,au->cxbu", grid_view, cos_first)
        first_imag = -contract("cxab,au->cxbu", grid_view, sin_first)
        bent_real, bent_imag = twist_phase(
            first_real, first_imag, cos_twist * norm_dip, sin_twist * norm_dip, -1.0
        )
        out_real, out_imag = pair_section(
            bent_real, bent_imag, "cxbi,bs->csix", cos_outer, sin_outer, -1.0
        )
        dip_spec = jnp.stack([out_real, out_imag], axis=1).reshape(3, 2, dip_block, row_count)
        return strike_forward(
            lax.all_to_all(dip_spec, "strike", split_axis=2, concat_axis=3, tiled=True)
        )

    def to_space(mode_field):
        mixed_rows = strike_inverse(mode_field)
        dip_spec = lax.all_to_all(mixed_rows, "strike", split_axis=3, concat_axis=2, tiled=True)
        gathered = lax.all_gather(dip_spec, "dip", axis=2, tiled=True)
        grid_view = gathered.reshape(3, 2, dip_count, strike_count, mode_rows, row_count)
        cos_last, sin_last = phase_table(coarse_own, coarse_all, unit_modes)
        first_real, first_imag = pair_section(
            grid_view[:, 0], grid_view[:, 1], "cdsix,bs->cxbdi", cos_outer, sin_outer, 1.0
        )
        first_real = first_real.reshape(3, row_count, strike_count, unit_modes)
        first_imag = first_imag.reshape(3, row_count, strike_count, unit_modes)
        cos_twist, sin_twist = phase_table(outer_index, coarse_all, dip_cells)
        bent_real, bent_imag = twist_phase(
            first_real, first_imag, cos_twist * norm_dip, sin_twist * norm_dip, 1.0
        )
        space_part = contract("cxbu,au->cxab", bent_real, cos_last) - contract(
            "cxbu,au->cxab", bent_imag, sin_last
        )
        return space_part.reshape(3, row_count, dip_block)

    def transfer(recent):
        recent_count = len(recent)
        summed = jnp.zeros(recent[0].shape, jnp.float32)
        for offset in range(HIST):
            if offset < recent_count:
                source = recent[offset]
            else:
                source = history[offset - recent_count].astype(jnp.float32)
            active = (offset < lengths).astype(jnp.float32)
            summed = summed + delay_term(source, delay_mixing(geometry, float(offset)), active)
        return summed

    first_spec = to_modes(slip_rate)
    force_field = to_space(transfer([first_spec]))
    next_rates, next_state = friction_step(
        force_field, prestress, normal_stress, direct_effect, state_log
    )
    second_spec = to_modes(next_rates)
    force_field = to_space(transfer([second_spec, first_spec]))
    next_rates, next_state = friction_step(
        force_field, prestress, normal_stress, direct_effect, next_state
    )
    return (next_rates, next_state)


def solution(mesh):
    return jax.shard_map(
        shards,
        mesh=mesh,
        in_specs=(
            P(None, "strike", "dip"),
            P(None, None, None, ("strike", "dip"), None),
            P(("strike", "dip"), None),
            P(None, "strike", "dip"),
            P("strike", "dip"),
            P("strike", "dip"),
            P("strike", "dip"),
        ),
        out_specs=(P(None, "strike", "dip"), P("strike", "dip")),
        check_vma=False,
    )
```

profile of v0, /device:TPU:1, one launch (start us, length us, event | category | flops | bytes accessed | tf_op | source)
XLA Modules:
  0.0 520.3 jit_solution(6019969516380714102)
XLA Ops:
  7.3 13.1 %all_gather.12 = f32[3,64,1024]{2,1,0:T(8,128)S(1)} all-gather(f32[3,64,256]{2,1,0:T(8,128)} %param.7), channel_id=1, replica_groups=mesh['strike'=64,'dip'=4] {'dip'}, dimensions={2}, use_global_device_ids=true | all-gather | bytes 983040 | tf_op jit(solution)/shard_map/all_gather | solution.py:158
  31.2 13.9 %all-to-all-start = ((f32[64,1,1536]{2,1,0:T(1,128)}), f32[64,1,1536]{2,1,0:T(1,128)S(1)}, u32[]{:S(2)}, u32[]{:S(2)}) async-start(f32[64,1,1536]{2,1,0:T(1,128)} %reshape.1792), calls=%async_computation | async-start | bytes 786432 | tf_op jit(solution)/shard_map/all_to_all | solution.py:172
  45.9 4.1 multiply_add_fusion.20
  60.7 2.8 multiply_add_fusion.5
  84.6 10.5 %copy.366 = f32[3,1,4,4096]{2,1,0,3:T(1,128)} copy(f32[3,1,4,4096]{3,2,0,1:T(4,128)S(1)} %stack.171) | data formatting | bytes 393216 | tf_op jit(solution)/shard_map/stack | solution.py:155
  96.7 10.3 %copy.367 = f32[3,1,4,4096]{2,1,0,3:T(1,128)} copy(f32[3,1,4,4096]{3,2,0,1:T(4,128)S(1)} %stack.172) | data formatting | bytes 393216 | tf_op jit(solution)/shard_map/stack | solution.py:155
  107.0 16.7 %fusion.506 = f32[4096,3,2,4]{3,2,1,0:T(2,128)} fusion(f32[3,1,4,4096]{2,1,0,3:T(1,128)} %copy.367, f32[3,1,4,4096]{2,1,0,3:T(1,128)} %copy.366), kind=kLoop, calls=%fused_computation.664 | loop fusion | flops 98304 | bytes 786432
  123.7 16.7 %reshape.1794 = f32[64,1,1536]{2,1,0:T(1,128)S(1)} reshape(f32[4096,3,2,4]{3,2,1,0:T(2,128)} %fusion.506) | data formatting | bytes 786432
  140.4 24.7 %all_to_all.66 = f32[64,1,1536]{2,1,0:T(1,128)S(1)} all-to-all(f32[64,1,1536]{2,1,0:T(1,128)S(1)} %reshape.1794), channel_id=1, replica_groups=mesh['strike'=64,'dip'=4] {'strike'}, dimensions={0} | all-to-all | bytes 786432 | tf_op jit(solution)/shard_map/all_to_all | solution.py:177
  166.7 21.1 %reshape.1795 = f32[4096,3,2,4]{3,2,1,0:T(2,128)} reshape(f32[64,1536]{1,0:T(8,128)S(1)} %reduce.1) | data formatting | bytes 786432
  187.8 16.1 %copy.455 = f32[3,2,4,64,64]{4,3,2,1,0:T(8,128)S(1)} copy(f32[3,2,4,64,64]{2,1,0,4,3:T(2,128)} %bitcast.476) | data formatting | bytes 786432 | tf_op jit(solution)/shard_map/all_to_all | solution.py:177
  205.5 38.9 %all-gather.3.cloned.1.call-done = f32[3,2,1024,64]{3,2,1,0:T(8,128)} async-done(((f32[3,2,256,64]{3,2,1,0:T(8,128)}), f32[3,2,1024,64]{3,2,1,0:T(8,128)}) %all-gather.3.cloned.1.call-update) | async-done | bytes 1572880 | tf_op jit(solution)/shard_map/all_gather | solution.py:178
  244.4 2.1 fusion.502
  248.2 2.8 fusion.16
  251.0 2.8 convolution_add_fusion.1
  255.9 4.2 convolution_subtract_fusion.1
  267.3 10.6 %all_gather.14 = f32[3,64,1024]{2,1,0:T(8,128)S(1)} all-gather(f32[3,64,256]{2,1,0:T(8,128)S(1)} %pad_maximum_fusion.6), channel_id=1, replica_groups=mesh['strike'=64,'dip'=4] {'dip'}, dimensions={2}, use_global_device_ids=true | all-gather | bytes 983040 | tf_op jit(solution)/shard_map/all_gather | solution.py:158
  288.9 14.7 %all-to-all-start.2 = ((f32[64,1,1536]{2,1,0:T(1,128)}), f32[64,1,1536]{2,1,0:T(1,128)S(1)}, u32[]{:S(2)}, u32[]{:S(2)}) async-start(f32[64,1,1536]{2,1,0:T(1,128)} %reshape.1796), calls=%async_computation.2 | async-start | bytes 786432 | tf_op jit(solution)/shard_map/all_to_all | solution.py:172
  307.8 10.3 %all-to-all-done.2 = f32[64,1,1536]{2,1,0:T(1,128)S(1)} async-done(((f32[64,1,1536]{2,1,0:T(1,128)}), f32[64,1,1536]{2,1,0:T(1,128)S(1)}, u32[]{:S(2)}, u32[]{:S(2)}) %all-to-all-start.2) | async-done | bytes 393248 | tf_op jit(solution)/shard_map/all_to_all | solution.py:172
  336.6 10.3 %copy.396 = f32[3,1,4,4096]{2,1,0,3:T(1,128)} copy(f32[3,1,4,4096]{3,2,0,1:T(4,128)S(1)} %stack.193) | data formatting | bytes 393216 | tf_op jit(solution)/shard_map/stack | solution.py:155
  348.6 10.3 %copy.397 = f32[3,1,4,4096]{2,1,0,3:T(1,128)} copy(f32[3,1,4,4096]{3,2,0,1:T(4,128)S(1)} %stack.194) | data formatting | bytes 393216 | tf_op jit(solution)/shard_map/stack | solution.py:155
  358.8 16.7 %fusion.505 = f32[4096,3,2,4]{3,2,1,0:T(2,128)} fusion(f32[3,1,4,4096]{2,1,0,3:T(1,128)} %copy.397, f32[3,1,4,4096]{2,1,0,3:T(1,128)} %copy.396), kind=kLoop, calls=%fused_computation.663 | loop fusion | flops 98304 | bytes 786432
  375.5 16.7 %reshape.1798 = f32[64,1,1536]{2,1,0:T(1,128)S(1)} reshape(f32[4096,3,2,4]{3,2,1,0:T(2,128)} %fusion.505) | data formatting | bytes 786432
  392.3 20.6 %all_to_all.67 = f32[64,1,1536]{2,1,0:T(1,128)S(1)} all-to-all(f32[64,1,1536]{2,1,0:T(1,128)S(1)} %reshape.1798), channel_id=1, replica_groups=mesh['strike'=64,'dip'=4] {'strike'}, dimensions={0} | all-to-all | bytes 786432 | tf_op jit(solution)/shard_map/all_to_all | solution.py:177
  414.4 21.1 %reshape.1799 = f32[4096,3,2,4]{3,2,1,0:T(2,128)} reshape(f32[64,1536]{1,0:T(8,128)S(1)} %reduce.3) | data formatting | bytes 786432
  435.5 15.9 %copy.467 = f32[3,2,4,64,64]{4,3,2,1,0:T(8,128)S(1)} copy(f32[3,2,4,64,64]{2,1,0,4,3:T(2,128)} %bitcast.477) | data formatting | bytes 786432 | tf_op jit(solution)/shard_map/all_to_all | solution.py:177
  452.9 37.3 %all-gather.5.cloned.1.call-done = f32[3,2,1024,64]{3,2,1,0:T(8,128)} async-done(((f32[3,2,256,64]{3,2,1,0:T(8,128)}), f32[3,2,1024,64]{3,2,1,0:T(8,128)}) %all-gather.5.cloned.1.call-update) | async-done | bytes 1572880 | tf_op jit(solution)/shard_map/all_gather | solution.py:178
  490.2 2.1 fusion.501
  494.0 2.8 fusion.18
  496.8 2.8 convolution_add_fusion
  499.6 2.1 copy.403
  501.7 4.2 convolution_subtract_fusion
  (207 shorter events, 105.6 us)
Async XLA Ops:
  28.9 16.8 %copy-start.34 = (s32[4,4096]{1,0:T(4,128)S(1)}, s32[4,4096]{1,0:T(4,128)}, u32[]{:S(2)}) copy-start(s32[4,4096]{1,0:T(4,128)} %param.9) | copy-start | bytes 196612
  28.9 16.8 %copy-start.33 = (bf16[4,3,2,4,4096]{4,3,2,1,0:T(4,128)(2,1)S(1)}, bf16[4,3,2,4,4096]{4,3,2,1,0:T(4,128)(2,1)}, u32[]{:S(2)}) copy-start(bf16[4,3,2,4,4096]{4,3,2,1,0:T(4,128)(2,1)} %param.8) | copy-start | bytes 2359300
  31.2 32.3 %all-to-all-start = ((f32[64,1,1536]{2,1,0:T(1,128)}), f32[64,1,1536]{2,1,0:T(1,128)S(1)}, u32[]{:S(2)}, u32[]{:S(2)}) async-start(f32[64,1,1536]{2,1,0:T(1,128)} %reshape.1792), calls=%async_computation | async-start | bytes 786432 | tf_op jit(solution)/shard_map/all_to_all | solution.py:172
  45.1 199.3 %all-gather.3.cloned.1.call-start = ((), (), s32[]{:S(2)}) async-start(), calls=%async_computation.4 | async-start | bytes 3932160 | tf_op jit(solution)/shard_map/all_gather | solution.py:178
  63.5 11.3 %copy-start.7 = (f32[4,64,64]{2,1,0:T(8,128)}, f32[4,64,64]{2,1,0:T(8,128)S(1)}, u32[]{:S(2)}) copy-start(f32[4,64,64]{2,1,0:T(8,128)S(1)} %get-tuple-element.73) | copy-start | bytes 196612
  63.5 12.3 %copy-start.1 = (f32[4,64,64]{2,1,0:T(8,128)}, f32[4,64,64]{2,1,0:T(8,128)S(1)}, u32[]{:S(2)}) copy-start(f32[4,64,64]{2,1,0:T(8,128)S(1)} %get-tuple-element.55) | copy-start | bytes 196612
  63.5 12.3 %copy-start.3 = (f32[4,64,64]{2,1,0:T(8,128)}, f32[4,64,64]{2,1,0:T(8,128)S(1)}, u32[]{:S(2)}) copy-start(f32[4,64,64]{2,1,0:T(8,128)S(1)} %get-tuple-element.56) | copy-start | bytes 196612
  63.5 12.3 %copy-start.5 = (f32[4,64,64]{2,1,0:T(8,128)}, f32[4,64,64]{2,1,0:T(8,128)S(1)}, u32[]{:S(2)}) copy-start(f32[4,64,64]{2,1,0:T(8,128)S(1)} %get-tuple-element.58) | copy-start | bytes 196612
  74.8 1.9 copy-start.18
  75.8 1.5 copy-start.16
  75.8 1.6 copy-start.17
  263.4 1.4 copy-start
  286.6 17.2 %copy-start.29 = (f32[1,2,4,4096]{3,2,1,0:T(4,128)S(1)}, f32[1,2,4,4096]{3,2,1,0:T(4,128)}, u32[]{:S(2)}) copy-start(f32[1,2,4,4096]{3,2,1,0:T(4,128)} %get-tuple-element.48) | copy-start | bytes 393220
  287.3 16.8 %copy-start.28 = (f32[1,2,4,4096]{3,2,1,0:T(4,128)S(1)}, f32[1,2,4,4096]{3,2,1,0:T(4,128)}, u32[]{:S(2)}) copy-start(f32[1,2,4,4096]{3,2,1,0:T(4,128)} %get-tuple-element.47) | copy-start | bytes 393220
  287.3 16.9 %copy-start.27 = (f32[1,2,4,4096]{3,2,1,0:T(4,128)S(1)}, f32[1,2,4,4096]{3,2,1,0:T(4,128)}, u32[]{:S(2)}) copy-start(f32[1,2,4,4096]{3,2,1,0:T(4,128)} %get-tuple-element.46) | copy-start | bytes 393220
  287.3 17.9 %copy-start.32 = (f32[1,2,4,4096]{3,2,1,0:T(4,128)S(1)}, f32[1,2,4,4096]{3,2,1,0:T(4,128)}, u32[]{:S(2)}) copy-start(f32[1,2,4,4096]{3,2,1,0:T(4,128)} %get-tuple-element.51) | copy-start | bytes 393220
  287.3 18.7 %copy-start.31 = (f32[1,2,4,4096]{3,2,1,0:T(4,128)S(1)}, f32[1,2,4,4096]{3,2,1,0:T(4,128)}, u32[]{:S(2)}) copy-start(f32[1,2,4,4096]{3,2,1,0:T(4,128)} %get-tuple-element.50) | copy-start | bytes 393220
  288.9 18.0 %copy-start.30 = (f32[1,2,4,4096]{3,2,1,0:T(4,128)S(1)}, f32[1,2,4,4096]{3,2,1,0:T(4,128)}, u32[]{:S(2)}) copy-start(f32[1,2,4,4096]{3,2,1,0:T(4,128)} %get-tuple-element.49) | copy-start | bytes 393220
  288.9 29.2 %all-to-all-start.2 = ((f32[64,1,1536]{2,1,0:T(1,128)}), f32[64,1,1536]{2,1,0:T(1,128)S(1)}, u32[]{:S(2)}, u32[]{:S(2)}) async-start(f32[64,1,1536]{2,1,0:T(1,128)} %reshape.1796), calls=%async_computation.2 | async-start | bytes 786432 | tf_op jit(solution)/shard_map/all_to_all | solution.py:172
  303.6 186.7 %all-gather.5.cloned.1.call-start = ((), (), s32[]{:S(2)}) async-start(), calls=%async_computation.5 | async-start | bytes 3932160 | tf_op jit(solution)/shard_map/all_gather | solution.py:178
  325.7 2.9 copy-start.2
  325.7 2.9 copy-start.4
  325.7 2.9 copy-start.6
  325.7 2.9 copy-start.8
  327.2 1.7 copy-start.9
  327.2 1.7 copy-start.19
  327.2 1.7 copy-start.20
  327.2 1.7 copy-start.21
  327.2 1.7 copy-start.22
  327.2 1.7 copy-start.23
  327.2 1.7 copy-start.24
  509.2 1.4 copy-start.26
  (7 other events, 7.7 us)
Sparse Core Ops, SparseCore 0:
  205.5 38.8 all-gather.2
  453.0 37.1 all-gather.4
where the time goes:
time: 528 us; the launch traced here: 520 us
  local copies, waits for them, and re-layouts  189 us (36%)
  waiting for transfers between devices  86.6 us (16%)
  matrix products  75.4 us (14%)
  blocking collectives  69 us (13%)
  other arithmetic  56.3 us (11%)
  starting transfers between devices  29.3 us (6%)
  between operations  15.2 us (3%)
    unnamed x78, local copies, waits for them, and re-layouts  81.5 us
    all_gather x2, waiting for transfers between devices, to_space(): gathered = lax.all_gather(dip_spec, 'dip', axis=2, tiled=True)  76.3 us
    dot_general x56, matrix products, contract(): return jnp.einsum(pattern, first_operand, second_operand, precision=highest)  75.4 us
    all_to_all x2, blocking collectives, to_space(): lax.all_to_all(mixed_rows, 'strike', split_axis=3, concat_axis=2, tiled=T...  45.3 us
    another operation x8, local copies, waits for them, and re-layouts, strike_inverse(): jnp.stack([out_real, out_imag], axis=1)  42.1 us
    all_to_all x4, local copies, waits for them, and re-layouts, to_space(): lax.all_to_all(mixed_rows, 'strike', split_axis=3, concat_axis=2, tiled=T...  34.9 us
    unnamed x2, other arithmetic  33.4 us
    all_to_all x2, starting transfers between devices, to_modes(): lax.all_to_all(dip_spec, 'strike', split_axis=2, concat_axis=3, tiled=True)  28.6 us
  transfers between devices with their start and end apart: 4, of which 3 were waited for; matrix products, arithmetic and copies ran while one was open for 4% of the time, Pallas kernels for 0%

commit v1 on v0

--- a/solution.py
+++ b/solution.py
@@ -175,7 +175,9 @@
     def to_space(mode_field):
         mixed_rows = strike_inverse(mode_field)
         dip_spec = lax.all_to_all(mixed_rows, "strike", split_axis=3, concat_axis=2, tiled=True)
-        gathered = lax.all_gather(dip_spec, "dip", axis=2, tiled=True)
+        gathered = jnp.concatenate(
+            lax.all_to_all(jnp.stack([dip_spec] * lax.axis_size("dip")), "dip", 0, 0), axis=2
+        )
         grid_view = gathered.reshape(3, 2, dip_count, strike_count, mode_rows, row_count)
         cos_last, sin_last = phase_table(coarse_own, coarse_all, unit_modes)
         first_real, first_imag = pair_section(

time: 528 us -> 486 us (0.920)
  waiting for transfers between devices: 86.6 us -> 30.2 us
  blocking collectives: 69 us -> 92.9 us
  between operations: 15.2 us -> 1.92 us
    all_gather x2 -> x0, waiting for transfers between devices: 76.3 us -> none  [to_space(): gathered = lax.all_gather(dip_spec, 'dip', axis=2, tiled=True)]
    all_to_all x0 -> x1, blocking collectives: none -> 23 us  [to_space(): lax.all_to_all(jnp.stack([dip_spec] * lax.axis_size('dip')), 'dip', 0, 0)]
    all_to_all x0 -> x1, waiting for transfers between devices: none -> 20 us  [to_space(): lax.all_to_all(jnp.stack([dip_spec] * lax.axis_size('dip')), 'dip', 0, 0)]
  transfers between devices with their start and end apart: 4 -> 3, of which waited for: 3 -> 2; matrix products, arithmetic and copies ran while one was open for 4% -> 5% of each run, Pallas kernels for 0% -> 0%
where the time goes in v1:
time: 486 us; the launch traced here: 478 us
  local copies, waits for them, and re-layouts  192 us (40%)
  blocking collectives  92.9 us (19%)
  matrix products  75.1 us (15%)
  other arithmetic  56.3 us (12%)
  waiting for transfers between devices  30.2 us (6%)
  starting transfers between devices  29.5 us (6%)
    unnamed x78, local copies, waits for them, and re-layouts  81.4 us
    dot_general x56, matrix products, contract(): return jnp.einsum(pattern, first_operand, second_operand, precision=highest)  75.1 us
    all_to_all x2, blocking collectives, to_space(): lax.all_to_all(mixed_rows, 'strike', split_axis=3, concat_axis=2, tiled=T...  45.3 us
    another operation x8, local copies, waits for them, and re-layouts, strike_inverse(): jnp.stack([out_real, out_imag], axis=1)  42.1 us
    unnamed x2, other arithmetic  33.4 us
    all_to_all x4, local copies, waits for them, and re-layouts, to_space(): lax.all_to_all(mixed_rows, 'strike', split_axis=3, concat_axis=2, tiled=T...  32.5 us
    all_to_all x2, starting transfers between devices, to_modes(): lax.all_to_all(dip_spec, 'strike', split_axis=2, concat_axis=3, tiled=True)  24.9 us
    all_gather x2, blocking collectives, to_modes(): gathered = lax.all_gather(space_field, 'dip', axis=2, tiled=True)  24.7 us
  transfers between devices with their start and end apart: 3, of which 2 were waited for; matrix products, arithmetic and copies ran while one was open for 5% of the time, Pallas kernels for 0%

profile of v1, /device:TPU:1, one launch (start us, length us, event | category | flops | bytes accessed | tf_op | source)
XLA Modules:
  0.0 478.3 jit_solution(863347101783896501)
XLA Ops:
  0.8 13.1 %all_gather.6 = f32[3,64,1024]{2,1,0:T(8,128)S(1)} all-gather(f32[3,64,256]{2,1,0:T(8,128)} %param.7), channel_id=1, replica_groups=mesh['strike'=64,'dip'=4] {'dip'}, dimensions={2}, use_global_device_ids=true | all-gather | bytes 983040 | tf_op jit(solution)/shard_map/all_gather | solution.py:158
  24.6 14.4 %all-to-all-start = ((f32[64,1,1536]{2,1,0:T(1,128)}), f32[64,1,1536]{2,1,0:T(1,128)S(1)}, u32[]{:S(2)}, u32[]{:S(2)}) async-start(f32[64,1,1536]{2,1,0:T(1,128)} %reshape.1798), calls=%async_computation | async-start | bytes 786432 | tf_op jit(solution)/shard_map/all_to_all | solution.py:172
  39.3 4.1 multiply_add_fusion.20
  54.1 2.8 multiply_add_fusion.5
  77.9 10.6 %copy.378 = f32[3,1,4,4096]{2,1,0,3:T(1,128)} copy(f32[3,1,4,4096]{3,2,0,1:T(4,128)S(1)} %stack.189) | data formatting | bytes 393216 | tf_op jit(solution)/shard_map/stack | solution.py:155
  90.1 10.2 %copy.379 = f32[3,1,4,4096]{2,1,0,3:T(1,128)} copy(f32[3,1,4,4096]{3,2,0,1:T(4,128)S(1)} %stack.190) | data formatting | bytes 393216 | tf_op jit(solution)/shard_map/stack | solution.py:155
  100.3 16.7 %fusion.506 = f32[4096,3,2,4]{3,2,1,0:T(2,128)} fusion(f32[3,1,4,4096]{2,1,0,3:T(1,128)} %copy.379, f32[3,1,4,4096]{2,1,0,3:T(1,128)} %copy.378), kind=kLoop, calls=%fused_computation.664 | loop fusion | flops 98304 | bytes 786432
  117.0 16.7 %reshape.1800 = f32[64,1,1536]{2,1,0:T(1,128)S(1)} reshape(f32[4096,3,2,4]{3,2,1,0:T(2,128)} %fusion.506) | data formatting | bytes 786432
  133.8 24.7 %all_to_all.70 = f32[64,1,1536]{2,1,0:T(1,128)S(1)} all-to-all(f32[64,1,1536]{2,1,0:T(1,128)S(1)} %reshape.1800), channel_id=1, replica_groups=mesh['strike'=64,'dip'=4] {'strike'}, dimensions={0} | all-to-all | bytes 786432 | tf_op jit(solution)/shard_map/all_to_all | solution.py:177
  160.0 21.1 %reshape.1801 = f32[4096,3,2,4]{3,2,1,0:T(2,128)} reshape(f32[64,1536]{1,0:T(8,128)S(1)} %reduce.1) | data formatting | bytes 786432
  181.1 15.7 %copy.471 = f32[3,2,4,64,64]{4,3,2,1,0:T(8,128)S(1)} copy(f32[3,2,4,64,64]{2,1,0,4,3:T(2,128)} %bitcast.480) | data formatting | bytes 786432 | tf_op jit(solution)/shard_map/all_to_all | solution.py:177
  199.0 4.6 all-to-all-start.2
  203.6 20.0 %all-to-all-done.2 = f32[4,3,2,256,64]{3,4,2,1,0:T(8,128)S(1)} async-done(((f32[4,3,2,256,64]{3,4,2,1,0:T(8,128)}), f32[4,3,2,256,64]{3,4,2,1,0:T(8,128)S(1)}, u32[]{:S(2)}, u32[]{:S(2)}) %all-to-all-start.2) | async-done | bytes 1572896 | tf_op jit(solution)/shard_map/all_to_all | solution.py:179
  223.6 2.2 copy.383
  229.7 2.8 fusion.16
  232.4 2.8 convolution_add_fusion.1
  237.4 4.2 convolution_subtract_fusion.1
  248.8 11.6 %all_gather.7 = f32[3,64,1024]{2,1,0:T(8,128)S(1)} all-gather(f32[3,64,256]{2,1,0:T(8,128)S(1)} %pad_maximum_fusion.6), channel_id=1, replica_groups=mesh['strike'=64,'dip'=4] {'dip'}, dimensions={2}, use_global_device_ids=true | all-gather | bytes 983040 | tf_op jit(solution)/shard_map/all_gather | solution.py:158
  271.3 10.6 %all-to-all-start.3 = ((f32[64,1,1536]{2,1,0:T(1,128)}), f32[64,1,1536]{2,1,0:T(1,128)S(1)}, u32[]{:S(2)}, u32[]{:S(2)}) async-start(f32[64,1,1536]{2,1,0:T(1,128)} %reshape.1802), calls=%async_computation.3 | async-start | bytes 786432 | tf_op jit(solution)/shard_map/all_to_all | solution.py:172
  285.9 10.1 %all-to-all-done.3 = f32[64,1,1536]{2,1,0:T(1,128)S(1)} async-done(((f32[64,1,1536]{2,1,0:T(1,128)}), f32[64,1,1536]{2,1,0:T(1,128)S(1)}, u32[]{:S(2)}, u32[]{:S(2)}) %all-to-all-start.3) | async-done | bytes 393248 | tf_op jit(solution)/shard_map/all_to_all | solution.py:172
  314.2 10.4 %copy.410 = f32[3,1,4,4096]{2,1,0,3:T(1,128)} copy(f32[3,1,4,4096]{3,2,0,1:T(4,128)S(1)} %stack.213) | data formatting | bytes 393216 | tf_op jit(solution)/shard_map/stack | solution.py:155
  326.1 10.2 %copy.411 = f32[3,1,4,4096]{2,1,0,3:T(1,128)} copy(f32[3,1,4,4096]{3,2,0,1:T(4,128)S(1)} %stack.214) | data formatting | bytes 393216 | tf_op jit(solution)/shard_map/stack | solution.py:155
  336.4 16.7 %fusion.505 = f32[4096,3,2,4]{3,2,1,0:T(2,128)} fusion(f32[3,1,4,4096]{2,1,0,3:T(1,128)} %copy.411, f32[3,1,4,4096]{2,1,0,3:T(1,128)} %copy.410), kind=kLoop, calls=%fused_computation.663 | loop fusion | flops 98304 | bytes 786432
  353.1 16.7 %reshape.1804 = f32[64,1,1536]{2,1,0:T(1,128)S(1)} reshape(f32[4096,3,2,4]{3,2,1,0:T(2,128)} %fusion.505) | data formatting | bytes 786432
  369.8 20.6 %all_to_all.71 = f32[64,1,1536]{2,1,0:T(1,128)S(1)} all-to-all(f32[64,1,1536]{2,1,0:T(1,128)S(1)} %reshape.1804), channel_id=1, replica_groups=mesh['strike'=64,'dip'=4] {'strike'}, dimensions={0} | all-to-all | bytes 786432 | tf_op jit(solution)/shard_map/all_to_all | solution.py:177
  392.0 21.1 %reshape.1805 = f32[4096,3,2,4]{3,2,1,0:T(2,128)} reshape(f32[64,1536]{1,0:T(8,128)S(1)} %reduce.3) | data formatting | bytes 786432
  413.1 15.7 %copy.483 = f32[3,2,4,64,64]{4,3,2,1,0:T(8,128)S(1)} copy(f32[3,2,4,64,64]{2,1,0,4,3:T(2,128)} %bitcast.481) | data formatting | bytes 786432 | tf_op jit(solution)/shard_map/all_to_all | solution.py:177
  429.8 23.0 %all_to_all.72 = f32[4,3,2,256,64]{3,4,2,1,0:T(8,128)S(1)} all-to-all(f32[4,3,2,256,64]{3,4,2,1,0:T(8,128)S(1)} %stack.217), channel_id=1, replica_groups=mesh['strike'=64,'dip'=4] {'dip'}, dimensions={0} | all-to-all | bytes 3145728 | tf_op jit(solution)/shard_map/all_to_all | solution.py:179
  452.8 2.2 copy.415
  458.8 2.8 fusion.18
  461.6 2.8 convolution_add_fusion
  466.5 4.2 convolution_subtract_fusion
  (210 shorter events, 110.9 us)
Async XLA Ops:
  22.4 16.7 %copy-start.34 = (s32[4,4096]{1,0:T(4,128)S(1)}, s32[4,4096]{1,0:T(4,128)}, u32[]{:S(2)}) copy-start(s32[4,4096]{1,0:T(4,128)} %param.9) | copy-start | bytes 196612
  22.4 16.8 %copy-start.33 = (bf16[4,3,2,4,4096]{4,3,2,1,0:T(4,128)(2,1)S(1)}, bf16[4,3,2,4,4096]{4,3,2,1,0:T(4,128)(2,1)}, u32[]{:S(2)}) copy-start(bf16[4,3,2,4,4096]{4,3,2,1,0:T(4,128)(2,1)} %param.8) | copy-start | bytes 2359300
  24.6 32.3 %all-to-all-start = ((f32[64,1,1536]{2,1,0:T(1,128)}), f32[64,1,1536]{2,1,0:T(1,128)S(1)}, u32[]{:S(2)}, u32[]{:S(2)}) async-start(f32[64,1,1536]{2,1,0:T(1,128)} %reshape.1798), calls=%async_computation | async-start | bytes 786432 | tf_op jit(solution)/shard_map/all_to_all | solution.py:172
  56.9 11.2 %copy-start.7 = (f32[4,64,64]{2,1,0:T(8,128)}, f32[4,64,64]{2,1,0:T(8,128)S(1)}, u32[]{:S(2)}) copy-start(f32[4,64,64]{2,1,0:T(8,128)S(1)} %get-tuple-element.73) | copy-start | bytes 196612
  56.9 12.3 %copy-start.1 = (f32[4,64,64]{2,1,0:T(8,128)}, f32[4,64,64]{2,1,0:T(8,128)S(1)}, u32[]{:S(2)}) copy-start(f32[4,64,64]{2,1,0:T(8,128)S(1)} %get-tuple-element.55) | copy-start | bytes 196612
  56.9 12.3 %copy-start.3 = (f32[4,64,64]{2,1,0:T(8,128)}, f32[4,64,64]{2,1,0:T(8,128)S(1)}, u32[]{:S(2)}) copy-start(f32[4,64,64]{2,1,0:T(8,128)S(1)} %get-tuple-element.56) | copy-start | bytes 196612
  56.9 12.3 %copy-start.5 = (f32[4,64,64]{2,1,0:T(8,128)}, f32[4,64,64]{2,1,0:T(8,128)S(1)}, u32[]{:S(2)}) copy-start(f32[4,64,64]{2,1,0:T(8,128)S(1)} %get-tuple-element.58) | copy-start | bytes 196612
  68.1 1.9 copy-start.18
  69.1 1.4 copy-start.15
  69.1 1.5 copy-start.16
  69.1 1.6 copy-start.17
  199.0 24.7 %all-to-all-start.2 = ((f32[4,3,2,256,64]{3,4,2,1,0:T(8,128)}), f32[4,3,2,256,64]{3,4,2,1,0:T(8,128)S(1)}, u32[]{:S(2)}, u32[]{:S(2)}) async-start(f32[4,3,2,256,64]{3,4,2,1,0:T(8,128)} %stack.193), calls=%async_computation.2 | async-start | bytes 3145728 | tf_op jit(solution)/shard_map/all_to_all | solution.py:179
  244.8 1.4 copy-start
  269.0 12.8 %copy-start.29 = (f32[1,2,4,4096]{3,2,1,0:T(4,128)S(1)}, f32[1,2,4,4096]{3,2,1,0:T(4,128)}, u32[]{:S(2)}) copy-start(f32[1,2,4,4096]{3,2,1,0:T(4,128)} %get-tuple-element.48) | copy-start | bytes 393220
  269.6 12.4 %copy-start.28 = (f32[1,2,4,4096]{3,2,1,0:T(4,128)S(1)}, f32[1,2,4,4096]{3,2,1,0:T(4,128)}, u32[]{:S(2)}) copy-start(f32[1,2,4,4096]{3,2,1,0:T(4,128)} %get-tuple-element.47) | copy-start | bytes 393220
  269.7 12.6 %copy-start.27 = (f32[1,2,4,4096]{3,2,1,0:T(4,128)S(1)}, f32[1,2,4,4096]{3,2,1,0:T(4,128)}, u32[]{:S(2)}) copy-start(f32[1,2,4,4096]{3,2,1,0:T(4,128)} %get-tuple-element.46) | copy-start | bytes 393220
  269.7 13.5 %copy-start.32 = (f32[1,2,4,4096]{3,2,1,0:T(4,128)S(1)}, f32[1,2,4,4096]{3,2,1,0:T(4,128)}, u32[]{:S(2)}) copy-start(f32[1,2,4,4096]{3,2,1,0:T(4,128)} %get-tuple-element.51) | copy-start | bytes 393220
  269.7 14.4 %copy-start.31 = (f32[1,2,4,4096]{3,2,1,0:T(4,128)S(1)}, f32[1,2,4,4096]{3,2,1,0:T(4,128)}, u32[]{:S(2)}) copy-start(f32[1,2,4,4096]{3,2,1,0:T(4,128)} %get-tuple-element.50) | copy-start | bytes 393220
  271.3 13.7 %copy-start.30 = (f32[1,2,4,4096]{3,2,1,0:T(4,128)S(1)}, f32[1,2,4,4096]{3,2,1,0:T(4,128)}, u32[]{:S(2)}) copy-start(f32[1,2,4,4096]{3,2,1,0:T(4,128)} %get-tuple-element.49) | copy-start | bytes 393220
  271.3 24.7 %all-to-all-start.3 = ((f32[64,1,1536]{2,1,0:T(1,128)}), f32[64,1,1536]{2,1,0:T(1,128)S(1)}, u32[]{:S(2)}, u32[]{:S(2)}) async-start(f32[64,1,1536]{2,1,0:T(1,128)} %reshape.1802), calls=%async_computation.3 | async-start | bytes 786432 | tf_op jit(solution)/shard_map/all_to_all | solution.py:172
  303.6 2.9 copy-start.2
  303.6 2.9 copy-start.4
  303.6 2.9 copy-start.6
  303.6 2.9 copy-start.8
  305.0 1.7 copy-start.9
  305.0 1.7 copy-start.19
  305.0 1.7 copy-start.20
  305.0 1.7 copy-start.21
  305.1 1.7 copy-start.22
  305.1 1.7 copy-start.23
  305.1 1.7 copy-start.24
  473.9 1.4 copy-start.26
  (6 other events, 6.3 us)
